TPU v7x, 32 devices: a whole 2x2x4 slice. The times are simulated.
32 devices in a mesh: expert: 8 (over z, core), tensor: 4 (over y, x).
Axes of the slice: x: 2, y: 2, z: 4, core: 2. Of those that a mesh axis runs over, the one named last changes fastest.
Arguments:
- tokens: bfloat16 [256, 4096], P('expert', 'tensor'), may hold values from -6 to 6
- cotangent: bfloat16 [256, 4096], P('expert', 'tensor'), may hold values from -6 to 6
- expert_ids: int32 [256, 8], P('expert'), may hold values from 0 to 63, all different within a row; in each aligned block of 32 rows (0 to 31, 32 to 63, ...) at most 8 rows name the same one
- route_weight: float32 [256, 8], P('expert'), may hold values from 0.05 to 0.25
- w_gate: bfloat16 [64, 4096, 1536], P('expert', 'tensor'), may hold values from -0.09375 to 0.09375
- w_up: bfloat16 [64, 4096, 1536], P('expert', 'tensor'), may hold values from -0.09375 to 0.09375
- w_down: bfloat16 [64, 1536, 4096], P('expert', None, 'tensor'), may hold values from -0.15625 to 0.15625
Outputs:
- mixed_out: bfloat16 [256, 4096], P('expert', 'tensor')
- input_grad: bfloat16 [256, 4096], P('expert', 'tensor')
- down_grad: bfloat16 [64, 1536, 4096], P('expert', None, 'tensor')
Inputs may be any that keep to these rules, and one draw needn't show every extreme that they name: `expert_ids`: each row names 8 different experts; within the 32 rows of one device no expert is named more than 8 times.
All inputs are finite; a program needn't handle non-finite values.
Results may differ from a plain program's by a relative error of at most 0.023.
Values may be sent and summed in bfloat16 or wider, within the bound.
No kernel may reach another device: no remote copies, remote signals or barrier semaphores. Data moves between devices by JAX's collectives and lax.ppermute only.
A program may use at most 192 MiB of HBM per device.

v0:
```python
import jax
import jax.numpy as jnp
from jax import lax
from jax.sharding import PartitionSpec as P


def local(tokens, cotangent, expert_ids, route_weight, w_gate, w_up, w_down):
    resident_specialists = w_gate.shape[0]
    experts = resident_specialists * lax.axis_size("expert")
    tok_count = expert_ids.shape[0]
    top_count = expert_ids.shape[1]
    capacity = 2 * tok_count * top_count // experts
    model_width = tokens.shape[1]
    flat_ids = expert_ids.reshape(-1)
    onehot = (flat_ids[:, None] == jnp.arange(experts, dtype=jnp.int32)[None, :]).astype(jnp.int32)
    before = jnp.cumsum(onehot, axis=0) - onehot
    slot_index = jnp.sum(before * onehot, axis=1)
    target = flat_ids * capacity + slot_index
    chosen = (target[:, None] == jnp.arange(experts * capacity, dtype=jnp.int32)[None, :]).astype(
        jnp.float32
    )
    chosen = chosen.reshape(tok_count, top_count, experts * capacity)
    expert_assignment = jnp.sum(chosen, axis=1)
    weighted = jnp.sum(chosen * route_weight[:, :, None], axis=1)
    token_send = jnp.dot(
        expert_assignment.T.astype(jnp.bfloat16), tokens, preferred_element_type=jnp.float32
    )
    token_send = token_send.astype(jnp.bfloat16).reshape(experts, capacity, model_width)
    gradient_outgoing = jnp.dot(
        weighted.T, cotangent, precision=lax.Precision.HIGHEST, preferred_element_type=jnp.float32
    )
    gradient_outgoing = gradient_outgoing.astype(jnp.bfloat16).reshape(
        experts, capacity, model_width
    )
    token_rows, grad_rows = (
        lax.all_to_all(token_send, "expert", split_axis=0, concat_axis=1, tiled=True),
        lax.all_to_all(gradient_outgoing, "expert", split_axis=0, concat_axis=1, tiled=True),
    )
    pre_gate = jnp.einsum("erd,edf->erf", token_rows, w_gate, preferred_element_type=jnp.float32)
    pre_up = jnp.einsum("erd,edf->erf", token_rows, w_up, preferred_element_type=jnp.float32)
    slice_breadth = w_gate.shape[2] // lax.axis_size("tensor")
    gate_sum, up_sum = (
        lax.psum(pre_gate.astype(jnp.bfloat16), "tensor").astype(jnp.float32),
        lax.psum(pre_up.astype(jnp.bfloat16), "tensor").astype(jnp.float32),
    )
    sigmoid_all = jax.nn.sigmoid(gate_sum)
    hidden = (gate_sum * sigmoid_all * up_sum).astype(jnp.bfloat16)
    out_rows = jnp.einsum(
        "erf,efd->erd", hidden, w_down, preferred_element_type=jnp.float32
    ).astype(jnp.bfloat16)
    down_grad = jnp.einsum("erf,erd->efd", hidden, grad_rows, preferred_element_type=jnp.float32)
    offset = lax.axis_index("tensor") * slice_breadth
    gate_part = lax.dynamic_slice_in_dim(gate_sum, offset, slice_breadth, 2)
    up_part = lax.dynamic_slice_in_dim(up_sum, offset, slice_breadth, 2)
    sigmoid_part = lax.dynamic_slice_in_dim(sigmoid_all, offset, slice_breadth, 2)
    hidden_term = jnp.einsum("erd,efd->erf", grad_rows, w_down, preferred_element_type=jnp.float32)
    hidden_grad = lax.psum_scatter(
        hidden_term.astype(jnp.bfloat16), "tensor", scatter_dimension=2, tiled=True
    ).astype(jnp.float32)
    gate_grad = (
        hidden_grad * up_part * sigmoid_part * (1.0 + gate_part * (1.0 - sigmoid_part))
    ).astype(jnp.bfloat16)
    up_grad = (hidden_grad * gate_part * sigmoid_part).astype(jnp.bfloat16)
    gate_piece = lax.all_gather(gate_grad, "tensor", axis=2, tiled=True)
    up_piece = lax.all_gather(up_grad, "tensor", axis=2, tiled=True)
    running = jnp.einsum("erf,edf->erd", gate_piece, w_gate, preferred_element_type=jnp.float32)
    input_rows = running + jnp.einsum(
        "erf,edf->erd", up_piece, w_up, preferred_element_type=jnp.float32
    )
    input_rows = input_rows.astype(jnp.bfloat16)
    returned_out, returned_in = (
        lax.all_to_all(out_rows, "expert", split_axis=1, concat_axis=0, tiled=True),
        lax.all_to_all(input_rows, "expert", split_axis=1, concat_axis=0, tiled=True),
    )
    returned_out = returned_out.reshape(experts * capacity, model_width)
    returned_in = returned_in.reshape(experts * capacity, model_width)
    mixed_out = jnp.dot(
        weighted, returned_out, precision=lax.Precision.HIGHEST, preferred_element_type=jnp.float32
    )
    input_grad = jnp.dot(
        expert_assignment.astype(jnp.bfloat16), returned_in, preferred_element_type=jnp.float32
    )
    return (
        mixed_out.astype(jnp.bfloat16),
        input_grad.astype(jnp.bfloat16),
        down_grad.astype(jnp.bfloat16),
    )


def solution(mesh):
    return jax.shard_map(
        local,
        mesh=mesh,
        in_specs=(
            P("expert", "tensor"),
            P("expert", "tensor"),
            P("expert", None),
            P("expert", None),
            P("expert", "tensor", None),
            P("expert", "tensor", None),
            P("expert", None, "tensor"),
        ),
        out_specs=(P("expert", "tensor"), P("expert", "tensor"), P("expert", None, "tensor")),
        check_vma=False,
    )
```

profile of v0, /device:TPU:0, one launch (start us, length us, event | category | flops | bytes accessed | tf_op | source)
XLA Modules:
  0.0 326.9 jit_solution(5938493697258200641)
XLA Ops:
  7.2 0.8 copy.45
  8.0 0.1 eq.43
  8.1 0.1 eq.39
  8.2 0.8 copy.49
  8.9 0.6 reduce-window.6
  9.6 0.2 slice_reduce_fusion
  9.8 0.1 fusion.17
  9.9 0.1 reduce_sum.30
  10.0 0.4 convert_reduce_fusion
  10.4 0.6 copy-done.4
  11.0 1.4 fusion
  12.4 6.4 %all-to-all-start = ((bf16[64,8,1024]{2,1,0:T(8,128)(2,1)}), bf16[64,8,1024]{2,1,0:T(8,128)(2,1)S(1)}, u32[]{:S(2)}, u32[]{:S(2)}) async-start(bf16[64,8,1024]{2,1,0:T(8,128)(2,1)} %fusion), calls=%async_computation | async-start | bytes 2097152 | tf_op jit(solution)/shard_map/all_to_all | solution.py:36
  18.8 2.0 fusion.1
  20.8 24.5 %all-to-all-done = bf16[64,8,1024]{2,1,0:T(8,128)(2,1)S(1)} async-done(((bf16[64,8,1024]{2,1,0:T(8,128)(2,1)}), bf16[64,8,1024]{2,1,0:T(8,128)(2,1)S(1)}, u32[]{:S(2)}, u32[]{:S(2)}) %all-to-all-start) | async-done | bytes 1048608 | tf_op jit(solution)/shard_map/all_to_all | solution.py:36
  45.4 3.6 %all-to-all-start.2 = ((bf16[64,8,1024]{2,1,0:T(8,128)(2,1)}), bf16[64,8,1024]{2,1,0:T(8,128)(2,1)S(1)}, u32[]{:S(2)}, u32[]{:S(2)}) async-start(bf16[64,8,1024]{2,1,0:T(8,128)(2,1)} %fusion.1), calls=%async_computation.2 | async-start | bytes 2097152 | tf_op jit(solution)/shard_map/all_to_all | solution.py:37
  48.9 0.0 all-reduce.3.cloned.1.call-start
  49.0 13.7 %convolution_convert_fusion.2 = bf16[8,64,1536]{2,1,0:T(8,128)(2,1)} fusion(bf16[8,1024,1536]{2,1,0:T(8,128)(2,1)} %param.12, bf16[8,8,8,1024]{3,2,1,0:T(8,128)(2,1)S(1)} %bitcast.68), kind=kOutput, calls=%fused_computation.4 | convolution fusion | flops 1611399168 | bytes 27787264 | tf_op jit(solution)/shard_map/erd,edf->erf/dot_general | solution.py:40
  62.7 13.7 %convolution_convert_fusion.3 = bf16[8,64,1536]{2,1,0:T(8,128)(2,1)} fusion(bf16[8,1024,1536]{2,1,0:T(8,128)(2,1)} %param.11, bf16[8,8,8,1024]{3,2,1,0:T(8,128)(2,1)S(1)} %bitcast.69), kind=kOutput, calls=%fused_computation.5 | convolution fusion | flops 1611399168 | bytes 27787264 | tf_op jit(solution)/shard_map/erd,edf->erf/dot_general | solution.py:39
  76.4 0.0 reduce-scatter.4.cloned.1.call-start
  76.5 13.2 %convolution_convert_fusion.1 = bf16[8,64,1536]{2,1,0:T(8,128)(2,1)S(1)} fusion(bf16[8,1536,1024]{2,1,0:T(8,128)(2,1)} %param.13, bf16[8,8,8,1024]{3,2,1,0:T(8,128)(2,1)S(1)} %bitcast.65), kind=kOutput, calls=%fused_computation.3 | convolution fusion | flops 1611399168 | bytes 27787264 | tf_op jit(solution)/shard_map/erd,efd->erf/dot_general | solution.py:56
  89.7 3.5 %copy.60 = bf16[8,64,1536]{1,0,2:T(8,128)(2,1)} copy(bf16[8,64,1536]{2,1,0:T(8,128)(2,1)S(1)} %convolution_convert_fusion.1) | data formatting | bytes 3145728
  93.2 5.4 %reshape.61 = bf16[1536,512]{1,0:T(8,128)(2,1)} reshape(bf16[1536,8,64]{2,1,0:T(8,128)(2,1)} %bitcast.67) | data formatting | bytes 3145728
  98.6 0.2 all-gather.3.cloned.1.call-start
  98.9 66.0 %all-reduce.3.cloned.1.call-done = (bf16[8,64,1536]{2,1,0:T(8,128)(2,1)}, bf16[8,64,1536]{2,1,0:T(8,128)(2,1)}) async-done(((bf16[8,64,1536]{2,1,0:T(8,128)(2,1)}, bf16[8,64,1536]{2,1,0:T(8,128)(2,1)}), (bf16[8,64,1536]{2,1,0:T(8,128)(2,1)}, bf16[8,64,1536]{2,1,0:T(8,128)(2,1)})) %all-reduce.3.cloned.1.call-update) | async-done | bytes 3145744 | tf_op jit(solution)/shard_map/psum | solution.py:43
  164.9 3.6 %convert_element_type.70 = f32[8,64,1536]{2,1,0:T(8,128)} convert(bf16[8,64,1536]{2,1,0:T(8,128)(2,1)} %get-tuple-element.5) | non-fusion elementwise | flops 786432 | bytes 4718592 | tf_op jit(solution)/shard_map/convert_element_type | solution.py:43
  168.5 2.5 add_divide_fusion
  171.0 28.1 %reduce-scatter.4.cloned.1.call-done = bf16[384,512]{1,0:T(8,128)(2,1)} async-done(((bf16[1536,512]{1,0:T(8,128)(2,1)}), bf16[384,512]{1,0:T(8,128)(2,1)}) %reduce-scatter.4.cloned.1.call-update) | async-done | bytes 393232
  199.0 1.5 reshape.62
  200.6 1.3 copy.61
  201.8 1.8 convert_element_type.72
  203.7 2.6 fusion.14
  206.3 0.0 all-gather.5.cloned.1.call-start
  206.4 0.5 all-gather.5.cloned.1.call-update
  206.9 13.5 %convolution_convert_fusion.4 = bf16[8,64,1024]{2,1,0:T(8,128)(2,1)S(1)} fusion(bf16[8,1536,1024]{2,1,0:T(8,128)(2,1)} %param.13, bf16[8,64,1536]{2,1,0:T(8,128)(2,1)S(1)} %copy-done.2, bf16[8,64,1536]{2,1,0:T(8,128)(2,1)} %get-tuple-element.6), kind=kOutput, calls=%fused_computation.7 | convolution fusion | flops 1617428480 | bytes 29360128 | tf_op jit(solution)/shard_map/erf,efd->erd/dot_general | solution.py:48
  220.4 1.6 copy.51
  222.0 4.6 %all-to-all-start.1 = ((bf16[8,64,1024]{2,0,1:T(8,128)(2,1)}), bf16[8,64,1024]{2,0,1:T(8,128)(2,1)}, u32[]{:S(2)}, u32[]{:S(2)}) async-start(bf16[8,64,1024]{2,0,1:T(8,128)(2,1)} %copy.51), calls=%async_computation.1 | async-start | bytes 2097152 | tf_op jit(solution)/shard_map/all_to_all | solution.py:72
  226.6 10.6 %all-gather.3.cloned.1.call-done = bf16[8,64,1536]{2,1,0:T(8,128)(2,1)} async-done(((bf16[8,64,384]{2,1,0:T(8,128)(2,1)}), bf16[8,64,1536]{2,1,0:T(8,128)(2,1)}) %all-gather.3.cloned.1.call-update) | async-done | bytes 1572880 | tf_op jit(solution)/shard_map/all_gather | solution.py:64
  237.2 13.8 %fusion.21 = f32[8,64,1024]{2,1,0:T(8,128)} fusion(bf16[8,64,1536]{2,1,0:T(8,128)(2,1)} %all-gather.3.cloned.1.call-done, bf16[8,1024,1536]{2,1,0:T(8,128)(2,1)} %param.11), kind=kOutput, calls=%fused_computation.44 | convolution fusion | flops 1610612736 | bytes 28835840 | tf_op jit(solution)/shard_map/erf,edf->erd/dot_general | solution.py:66
  251.0 18.6 %all-gather.5.cloned.1.call-done = bf16[8,64,1536]{2,1,0:T(8,128)(2,1)} async-done(((bf16[8,64,384]{2,1,0:T(8,128)(2,1)}), bf16[8,64,1536]{2,1,0:T(8,128)(2,1)}) %all-gather.5.cloned.1.call-update) | async-done | bytes 1572880 | tf_op jit(solution)/shard_map/all_gather | solution.py:65
  269.6 14.0 %add_convert_fusion = bf16[8,64,1024]{2,1,0:T(8,128)(2,1)} fusion(f32[8,64,1024]{2,1,0:T(8,128)} %fusion.21, bf16[8,64,1536]{2,1,0:T(8,128)(2,1)} %all-gather.5.cloned.1.call-done, bf16[8,1024,1536]{2,1,0:T(8,128)(2,1)} %param.12), kind=kOutput, calls=%fused_computation.6 | convolution fusion | flops 1611661312 | bytes 29884416 | tf_op jit(solution)/shard_map/erf,edf->erd/dot_general | solution.py:67
  283.6 2.8 copy.55
  286.3 4.6 %all-to-all-start.3 = ((bf16[8,64,1024]{2,0,1:T(8,128)(2,1)}), bf16[8,64,1024]{2,0,1:T(8,128)(2,1)}, u32[]{:S(2)}, u32[]{:S(2)}) async-start(bf16[8,64,1024]{2,0,1:T(8,128)(2,1)} %copy.55), calls=%async_computation.3 | async-start | bytes 2097152 | tf_op jit(solution)/shard_map/all_to_all | solution.py:73
  291.0 13.8 %convolution_convert_fusion = bf16[8,1536,1024]{2,1,0:T(8,128)(2,1)} fusion(bf16[8,8,8,1024]{3,2,1,0:T(8,128)(2,1)S(1)} %bitcast.66, bf16[8,64,1536]{2,1,0:T(8,128)(2,1)S(1)} %copy-done.2, bf16[8,64,1536]{2,1,0:T(8,128)(2,1)} %get-tuple-element.6), kind=kOutput, calls=%fused_computation | convolution fusion | flops 1629487104 | bytes 29360128 | tf_op jit(solution)/shard_map/erf,erd->efd/dot_general | solution.py:51
  304.8 1.9 copy.53
  306.6 1.2 convolution_convert_fusion.8
  307.9 9.8 %all-to-all-done.3 = bf16[8,64,1024]{2,0,1:T(8,128)(2,1)} async-done(((bf16[8,64,1024]{2,0,1:T(8,128)(2,1)}), bf16[8,64,1024]{2,0,1:T(8,128)(2,1)}, u32[]{:S(2)}, u32[]{:S(2)}) %all-to-all-start.3) | async-done | bytes 1048608 | tf_op jit(solution)/shard_map/all_to_all | solution.py:73
  317.6 1.8 copy.57
  319.5 0.9 convolution_convert_fusion.7
  (22 shorter events, 0.2 us)
Async XLA Ops:
  7.2 3.9 %copy-start = (bf16[32,1024]{1,0:T(8,128)(2,1)S(1)}, bf16[32,1024]{1,0:T(8,128)(2,1)}, u32[]{:S(2)}) copy-start(bf16[32,1024]{1,0:T(8,128)(2,1)} %param.7) | copy-start | bytes 196612
  7.2 11.6 %copy-start.6 = (bf16[32,1024]{1,0:T(8,128)(2,1)S(1)}, bf16[32,1024]{1,0:T(8,128)(2,1)}, u32[]{:S(2)}) copy-start(bf16[32,1024]{1,0:T(8,128)(2,1)} %param.8) | copy-start | bytes 196612
  10.4 0.6 copy-start.4
  12.4 32.9 %all-to-all-start = ((bf16[64,8,1024]{2,1,0:T(8,128)(2,1)}), bf16[64,8,1024]{2,1,0:T(8,128)(2,1)S(1)}, u32[]{:S(2)}, u32[]{:S(2)}) async-start(bf16[64,8,1024]{2,1,0:T(8,128)(2,1)} %fusion), calls=%async_computation | async-start | bytes 2097152 | tf_op jit(solution)/shard_map/all_to_all | solution.py:36
  45.4 31.1 %all-to-all-start.2 = ((bf16[64,8,1024]{2,1,0:T(8,128)(2,1)}), bf16[64,8,1024]{2,1,0:T(8,128)(2,1)S(1)}, u32[]{:S(2)}, u32[]{:S(2)}) async-start(bf16[64,8,1024]{2,1,0:T(8,128)(2,1)} %fusion.1), calls=%async_computation.2 | async-start | bytes 2097152 | tf_op jit(solution)/shard_map/all_to_all | solution.py:37
  48.9 116.0 %all-reduce.3.cloned.1.call-start = ((), (), s32[]{:S(2)}) async-start(), calls=%async_computation.8 | async-start | bytes 6291456 | tf_op jit(solution)/shard_map/psum | solution.py:43
  76.4 122.6 %reduce-scatter.4.cloned.1.call-start = ((), (), s32[]{:S(2)}) async-start(), calls=%async_computation.7 | async-start | bytes 1966080
  98.6 138.5 %all-gather.3.cloned.1.call-start = ((), (), s32[]{:S(2)}) async-start(), calls=%async_computation.5 | async-start | bytes 1966080 | tf_op jit(solution)/shard_map/all_gather | solution.py:64
  164.9 3.6 %copy-start.2 = (bf16[8,64,1536]{2,1,0:T(8,128)(2,1)S(1)}, bf16[8,64,1536]{2,1,0:T(8,128)(2,1)}, u32[]{:S(2)}) copy-start(bf16[8,64,1536]{2,1,0:T(8,128)(2,1)} %get-tuple-element.5) | copy-start | bytes 4718596
  201.8 1.9 copy-start.3
  206.3 63.3 %all-gather.5.cloned.1.call-start = ((), (), s32[]{:S(2)}) async-start(), calls=%async_computation.6 | async-start | bytes 1966080 | tf_op jit(solution)/shard_map/all_gather | solution.py:65
  222.0 64.3 %all-to-all-start.1 = ((bf16[8,64,1024]{2,0,1:T(8,128)(2,1)}), bf16[8,64,1024]{2,0,1:T(8,128)(2,1)}, u32[]{:S(2)}, u32[]{:S(2)}) async-start(bf16[8,64,1024]{2,0,1:T(8,128)(2,1)} %copy.51), calls=%async_computation.1 | async-start | bytes 2097152 | tf_op jit(solution)/shard_map/all_to_all | solution.py:72
  286.3 31.3 %all-to-all-start.3 = ((bf16[8,64,1024]{2,0,1:T(8,128)(2,1)}), bf16[8,64,1024]{2,0,1:T(8,128)(2,1)}, u32[]{:S(2)}, u32[]{:S(2)}) async-start(bf16[8,64,1024]{2,0,1:T(8,128)(2,1)} %copy.55), calls=%async_computation.3 | async-start | bytes 2097152 | tf_op jit(solution)/shard_map/all_to_all | solution.py:73
  304.8 14.7 %copy-start.5 = (bf16[32,512]{1,0:T(8,128)(2,1)S(1)}, bf16[32,512]{1,0:T(8,128)(2,1)}, u32[]{:S(2)}) copy-start(bf16[32,512]{1,0:T(8,128)(2,1)} %copy-done.4) | copy-start | bytes 98308
  304.8 15.6 %copy-start.1 = (bf16[32,1024]{1,0:T(8,128)(2,1)S(1)}, bf16[32,1024]{1,0:T(8,128)(2,1)}, u32[]{:S(2)}) copy-start(bf16[32,1024]{1,0:T(8,128)(2,1)} %param.7) | copy-start | bytes 196612
Sparse Core Ops, SparseCore 0:
  76.5 88.3 all-reduce.2
  167.9 31.1 reduce-scatter.3
  206.4 30.6 all-gather.2
  238.8 30.6 all-gather.4
where the time goes:
time: 328 us; the launch traced here: 327 us
  waiting for transfers between devices  158 us (48%)
  matrix products  101 us (31%)
  local copies, waits for them, and re-layouts  22.4 us (7%)
  starting transfers between devices  19.4 us (6%)
  between operations  13.9 us (4%)
  other arithmetic  11.7 us (4%)
    psum x1, waiting for transfers between devices, local(): lax.psum(pre_gate.astype(jnp.bfloat16), 'tensor').astype(jnp.float32)  66 us
    unnamed x5, waiting for transfers between devices  28.6 us
    all_to_all x1, waiting for transfers between devices, local(): lax.all_to_all(token_send, 'expert', split_axis=0, concat_axis=1, tiled=T...  24.5 us
    all_gather x1, waiting for transfers between devices, local(): up_piece = lax.all_gather(up_grad, 'tensor', axis=2, tiled=True)  18.6 us
    dot_general x1, matrix products, local(): jnp.einsum('erf,edf->erd', up_piece, w_up, preferred_element_type=jnp.flo...  14 us
    unnamed x20, local copies, waits for them, and re-layouts  13.9 us
    dot_general x1, matrix products, local(): jnp.einsum('erf,erd->efd', hidden, grad_rows, preferred_element_type=jnp....  13.8 us
    dot_general x1, matrix products, local(): jnp.einsum('erf,edf->erd', gate_piece, w_gate, preferred_element_type=jnp...  13.8 us
  transfers between devices with their start and end apart: 8, of which 6 were waited for; matrix products, arithmetic and copies ran while one was open for 37% of the time, Pallas kernels for 0%

commit v1 on v0

--- a/solution.py
+++ b/solution.py
@@ -40,7 +40,9 @@
     pre_up = jnp.einsum("erd,edf->erf", token_rows, w_up, preferred_element_type=jnp.float32)
     slice_breadth = w_gate.shape[2] // lax.axis_size("tensor")
     gate_sum, up_sum = (
-        lax.psum(pre_gate.astype(jnp.bfloat16), "tensor").astype(jnp.float32),
+        jnp.sum(lax.all_gather(pre_gate.astype(jnp.bfloat16), "tensor"), axis=0).astype(
+            jnp.float32
+        ),
         lax.psum(pre_up.astype(jnp.bfloat16), "tensor").astype(jnp.float32),
     )
     sigmoid_all = jax.nn.sigmoid(gate_sum)

time: 328 us -> 360 us (1.098)
  waiting for transfers between devices: 158 us -> 188 us
    all_gather x0 -> x1, waiting for transfers between devices: none -> 69.9 us  [local(): lax.all_gather(pre_gate.astype(jnp.bfloat16), 'tensor')]
    psum x1, waiting for transfers between devices: 66 us -> 11.2 us  [local(): lax.psum(pre_up.astype(jnp.bfloat16), 'tensor').astype(jnp.float32)]
    all_to_all x1, waiting for transfers between devices: 0.01 us -> 12.6 us  [local(): lax.all_to_all(gradient_outgoing, 'expert', split_axis=0, concat_axis=1,...]
    reduce_sum x0 -> x1, other arithmetic: none -> 4.03 us  [local(): jnp.sum(lax.all_gather(pre_gate.astype(jnp.bfloat16), 'tensor'), axis=0)]
    unnamed x5 -> x6, waiting for transfers between devices: 28.6 us -> 31.3 us
    unnamed x20 -> x12, local copies, waits for them, and re-layouts: 13.9 us -> 13.9 us
  transfers between devices with their start and end apart: 8 -> 9, of which waited for: 6 -> 8; matrix products, arithmetic and copies ran while one was open for 37% -> 34% of each run, Pallas kernels for 0% -> 0%
where the time goes in v1:
time: 360 us; the launch traced here: 359 us
  waiting for transfers between devices  188 us (52%)
  matrix products  102 us (28%)
  local copies, waits for them, and re-layouts  22.4 us (6%)
  starting transfers between devices  19.5 us (5%)
  between operations  13.9 us (4%)
  other arithmetic  12.3 us (3%)
    all_gather x1, waiting for transfers between devices, local(): lax.all_gather(pre_gate.astype(jnp.bfloat16), 'tensor')  69.9 us
    unnamed x6, waiting for transfers between devices  31.3 us
    all_to_all x1, waiting for transfers between devices, local(): lax.all_to_all(token_send, 'expert', split_axis=0, concat_axis=1, tiled=T...  24.5 us
    all_gather x1, waiting for transfers between devices, local(): up_piece = lax.all_gather(up_grad, 'tensor', axis=2, tiled=True)  18.6 us
    dot_general x1, matrix products, local(): jnp.einsum('erd,edf->erf', token_rows, w_gate, preferred_element_type=jnp...  14.1 us
    dot_general x1, matrix products, local(): jnp.einsum('erf,edf->erd', up_piece, w_up, preferred_element_type=jnp.flo...  14 us
    unnamed x12, local copies, waits for them, and re-layouts  13.9 us
    dot_general x1, matrix products, local(): jnp.einsum('erf,erd->efd', hidden, grad_rows, preferred_element_type=jnp....  13.8 us
  transfers between devices with their start and end apart: 9, of which 8 were waited for; matrix products, arithmetic and copies ran while one was open for 34% of the time, Pallas kernels for 0%

profile of v1, /device:TPU:0, one launch (start us, length us, event | category | flops | bytes accessed | tf_op | source)
XLA Modules:
  0.0 358.8 jit_solution(7566077223409970173)
XLA Ops:
  7.2 0.8 copy.45
  8.0 0.1 eq.43
  8.1 0.1 eq.39
  8.2 0.8 copy.49
  8.9 0.6 reduce-window.6
  9.6 0.2 slice_reduce_fusion
  9.8 0.1 fusion.17
  9.9 0.1 reduce_sum.42
  10.0 0.4 convert_reduce_fusion
  10.4 1.4 fusion
  11.8 6.4 %all-to-all-start = ((bf16[64,8,1024]{2,1,0:T(8,128)(2,1)}), bf16[64,8,1024]{2,1,0:T(8,128)(2,1)S(1)}, u32[]{:S(2)}, u32[]{:S(2)}) async-start(bf16[64,8,1024]{2,1,0:T(8,128)(2,1)} %fusion), calls=%async_computation | async-start | bytes 2097152 | tf_op jit(solution)/shard_map/all_to_all | solution.py:36
  18.2 2.0 fusion.1
  20.2 24.5 %all-to-all-done = bf16[64,8,1024]{2,1,0:T(8,128)(2,1)S(1)} async-done(((bf16[64,8,1024]{2,1,0:T(8,128)(2,1)}), bf16[64,8,1024]{2,1,0:T(8,128)(2,1)S(1)}, u32[]{:S(2)}, u32[]{:S(2)}) %all-to-all-start) | async-done | bytes 1048608 | tf_op jit(solution)/shard_map/all_to_all | solution.py:36
  44.8 3.6 all-to-all-start.2
  48.4 13.8 %convolution_convert_fusion.2 = bf16[8,64,1536]{2,1,0:T(8,128)(2,1)} fusion(bf16[8,1024,1536]{2,1,0:T(8,128)(2,1)} %param.12, bf16[8,8,8,1024]{3,2,1,0:T(8,128)(2,1)S(1)} %bitcast.69), kind=kOutput, calls=%fused_computation.4 | convolution fusion | flops 1611399168 | bytes 27787264 | tf_op jit(solution)/shard_map/erd,edf->erf/dot_general | solution.py:40
  62.2 12.6 %all-to-all-done.2 = bf16[64,8,1024]{2,1,0:T(8,128)(2,1)S(1)} async-done(((bf16[64,8,1024]{2,1,0:T(8,128)(2,1)}), bf16[64,8,1024]{2,1,0:T(8,128)(2,1)S(1)}, u32[]{:S(2)}, u32[]{:S(2)}) %all-to-all-start.2) | async-done | bytes 1048608 | tf_op jit(solution)/shard_map/all_to_all | solution.py:37
  74.8 13.8 %convolution_convert_fusion.1 = bf16[8,64,1536]{2,1,0:T(8,128)(2,1)} fusion(bf16[8,1536,1024]{2,1,0:T(8,128)(2,1)} %param.13, bf16[8,8,8,1024]{3,2,1,0:T(8,128)(2,1)S(1)} %bitcast.66), kind=kOutput, calls=%fused_computation.3 | convolution fusion | flops 1611399168 | bytes 27787264 | tf_op jit(solution)/shard_map/erd,efd->erf/dot_general | solution.py:58
  88.6 4.9 %copy.60 = bf16[8,64,1536]{1,0,2:T(8,128)(2,1)} copy(bf16[8,64,1536]{2,1,0:T(8,128)(2,1)} %convolution_convert_fusion.1) | data formatting | bytes 3145728
  93.4 5.4 %reshape.62 = bf16[1536,512]{1,0:T(8,128)(2,1)} reshape(bf16[1536,8,64]{2,1,0:T(8,128)(2,1)} %bitcast.68) | data formatting | bytes 3145728
  98.9 0.0 all-gather.9.cloned.1.call-start
  98.9 14.1 %convolution_convert_fusion.3 = bf16[8,64,1536]{2,1,0:T(8,128)(2,1)} fusion(bf16[8,1024,1536]{2,1,0:T(8,128)(2,1)} %param.11, bf16[8,8,8,1024]{3,2,1,0:T(8,128)(2,1)S(1)} %bitcast.70), kind=kOutput, calls=%fused_computation.5 | convolution fusion | flops 1611399168 | bytes 27787264 | tf_op jit(solution)/shard_map/erd,edf->erf/dot_general | solution.py:39
  113.0 0.2 all-gather.5.cloned.1.call-start
  113.2 11.2 %all-reduce.2.cloned.1.call-done = bf16[8,64,1536]{2,1,0:T(8,128)(2,1)} async-done(((bf16[8,64,1536]{2,1,0:T(8,128)(2,1)}), bf16[8,64,1536]{2,1,0:T(8,128)(2,1)}) %all-reduce.2.cloned.1.call-update) | async-done | bytes 1572880 | tf_op jit(solution)/shard_map/psum | solution.py:46
  124.4 3.5 convert_element_type.74
  127.9 30.7 %reduce-scatter.4.cloned.1.call-done = bf16[384,512]{1,0:T(8,128)(2,1)} async-done(((bf16[1536,512]{1,0:T(8,128)(2,1)}), bf16[384,512]{1,0:T(8,128)(2,1)}) %reduce-scatter.4.cloned.1.call-update) | async-done | bytes 393232
  158.6 1.5 reshape.63
  160.1 0.5 copy.61
  160.6 69.9 %all-gather.9.cloned.1.call-done = bf16[32,64,1536]{2,1,0:T(8,128)(2,1)} async-done(((bf16[8,64,1536]{2,1,0:T(8,128)(2,1)}), bf16[32,64,1536]{2,1,0:T(8,128)(2,1)}) %all-gather.9.cloned.1.call-update) | async-done | bytes 6291472 | tf_op jit(solution)/shard_map/all_gather | solution.py:43
  230.5 4.0 %reduce_sum.45 = bf16[8,64,1536]{2,1,0:T(8,128)(2,1)S(1)} reduce(bf16[4,8,64,1536]{3,2,1,0:T(8,128)(2,1)} %bitcast.71, bf16[]{:T(256)} %constant.7.clone.1), dimensions={0}, to_apply=%region_5.6 | reduce | flops 2359296 | bytes 7864322 | tf_op jit(solution)/shard_map/reduce_sum | solution.py:43
  234.5 0.8 add_divide_fusion
  235.3 0.4 convert_element_type.72
  235.7 2.4 fusion.14
  238.2 0.5 all-gather.7.cloned.1.call-update
  238.7 13.5 %convolution_convert_fusion.4 = bf16[8,64,1024]{2,1,0:T(8,128)(2,1)S(1)} fusion(bf16[8,1536,1024]{2,1,0:T(8,128)(2,1)} %param.13, bf16[8,64,1536]{2,1,0:T(8,128)(2,1)S(1)} %reduce_sum.45, bf16[8,64,1536]{2,1,0:T(8,128)(2,1)} %all-reduce.2.cloned.1.call-done), kind=kOutput, calls=%fused_computation.7 | convolution fusion | flops 1617428480 | bytes 29360128 | tf_op jit(solution)/shard_map/erf,efd->erd/dot_general | solution.py:50
  252.3 1.5 copy.51
  253.8 4.6 %all-to-all-start.1 = ((bf16[8,64,1024]{2,0,1:T(8,128)(2,1)}), bf16[8,64,1024]{2,0,1:T(8,128)(2,1)}, u32[]{:S(2)}, u32[]{:S(2)}) async-start(bf16[8,64,1024]{2,0,1:T(8,128)(2,1)} %copy.51), calls=%async_computation.1 | async-start | bytes 2097152 | tf_op jit(solution)/shard_map/all_to_all | solution.py:74
  258.4 10.6 %all-gather.5.cloned.1.call-done = bf16[8,64,1536]{2,1,0:T(8,128)(2,1)} async-done(((bf16[8,64,384]{2,1,0:T(8,128)(2,1)}), bf16[8,64,1536]{2,1,0:T(8,128)(2,1)}) %all-gather.5.cloned.1.call-update) | async-done | bytes 1572880 | tf_op jit(solution)/shard_map/all_gather | solution.py:66
  269.0 13.8 %fusion.21 = f32[8,64,1024]{2,1,0:T(8,128)} fusion(bf16[8,64,1536]{2,1,0:T(8,128)(2,1)} %all-gather.5.cloned.1.call-done, bf16[8,1024,1536]{2,1,0:T(8,128)(2,1)} %param.11), kind=kOutput, calls=%fused_computation.44 | convolution fusion | flops 1610612736 | bytes 28835840 | tf_op jit(solution)/shard_map/erf,edf->erd/dot_general | solution.py:68
  282.8 18.6 %all-gather.7.cloned.1.call-done = bf16[8,64,1536]{2,1,0:T(8,128)(2,1)} async-done(((bf16[8,64,384]{2,1,0:T(8,128)(2,1)}), bf16[8,64,1536]{2,1,0:T(8,128)(2,1)}) %all-gather.7.cloned.1.call-update) | async-done | bytes 1572880 | tf_op jit(solution)/shard_map/all_gather | solution.py:67
  301.4 14.0 %add_convert_fusion = bf16[8,64,1024]{2,1,0:T(8,128)(2,1)} fusion(f32[8,64,1024]{2,1,0:T(8,128)} %fusion.21, bf16[8,64,1536]{2,1,0:T(8,128)(2,1)} %all-gather.7.cloned.1.call-done, bf16[8,1024,1536]{2,1,0:T(8,128)(2,1)} %param.12), kind=kOutput, calls=%fused_computation.6 | convolution fusion | flops 1611661312 | bytes 29884416 | tf_op jit(solution)/shard_map/erf,edf->erd/dot_general | solution.py:69
  315.4 2.8 copy.55
  318.2 4.6 %all-to-all-start.3 = ((bf16[8,64,1024]{2,0,1:T(8,128)(2,1)}), bf16[8,64,1024]{2,0,1:T(8,128)(2,1)}, u32[]{:S(2)}, u32[]{:S(2)}) async-start(bf16[8,64,1024]{2,0,1:T(8,128)(2,1)} %copy.55), calls=%async_computation.3 | async-start | bytes 2097152 | tf_op jit(solution)/shard_map/all_to_all | solution.py:75
  322.8 13.8 %convolution_convert_fusion = bf16[8,1536,1024]{2,1,0:T(8,128)(2,1)} fusion(bf16[8,8,8,1024]{3,2,1,0:T(8,128)(2,1)S(1)} %bitcast.67, bf16[8,64,1536]{2,1,0:T(8,128)(2,1)S(1)} %reduce_sum.45, bf16[8,64,1536]{2,1,0:T(8,128)(2,1)} %all-reduce.2.cloned.1.call-done), kind=kOutput, calls=%fused_computation | convolution fusion | flops 1629487104 | bytes 29360128 | tf_op jit(solution)/shard_map/erf,erd->efd/dot_general | solution.py:53
  336.6 1.9 copy.53
  338.5 1.2 convolution_convert_fusion.8
  339.7 9.8 %all-to-all-done.3 = bf16[8,64,1024]{2,0,1:T(8,128)(2,1)} async-done(((bf16[8,64,1024]{2,0,1:T(8,128)(2,1)}), bf16[8,64,1024]{2,0,1:T(8,128)(2,1)}, u32[]{:S(2)}, u32[]{:S(2)}) %all-to-all-start.3) | async-done | bytes 1048608 | tf_op jit(solution)/shard_map/all_to_all | solution.py:75
  349.5 1.8 copy.57
  351.3 0.9 convolution_convert_fusion.7
  (18 shorter events, 0.3 us)
Async XLA Ops:
  7.2 3.2 copy-start
  7.2 11.0 %copy-start.2 = (bf16[32,1024]{1,0:T(8,128)(2,1)S(1)}, bf16[32,1024]{1,0:T(8,128)(2,1)}, u32[]{:S(2)}) copy-start(bf16[32,1024]{1,0:T(8,128)(2,1)} %param.8) | copy-start | bytes 196612
  11.8 32.9 %all-to-all-start = ((bf16[64,8,1024]{2,1,0:T(8,128)(2,1)}), bf16[64,8,1024]{2,1,0:T(8,128)(2,1)S(1)}, u32[]{:S(2)}, u32[]{:S(2)}) async-start(bf16[64,8,1024]{2,1,0:T(8,128)(2,1)} %fusion), calls=%async_computation | async-start | bytes 2097152 | tf_op jit(solution)/shard_map/all_to_all | solution.py:36
  44.8 30.1 %all-to-all-start.2 = ((bf16[64,8,1024]{2,1,0:T(8,128)(2,1)}), bf16[64,8,1024]{2,1,0:T(8,128)(2,1)S(1)}, u32[]{:S(2)}, u32[]{:S(2)}) async-start(bf16[64,8,1024]{2,1,0:T(8,128)(2,1)} %fusion.1), calls=%async_computation.2 | async-start | bytes 2097152 | tf_op jit(solution)/shard_map/all_to_all | solution.py:37
  48.3 76.1 %all-reduce.2.cloned.1.call-start = ((), (), s32[]{:S(2)}) async-start(), calls=%async_computation.5 | async-start | bytes 3145728 | tf_op jit(solution)/shard_map/psum | solution.py:46
  62.1 96.4 %reduce-scatter.4.cloned.1.call-start = ((), (), s32[]{:S(2)}) async-start(), calls=%async_computation.9 | async-start | bytes 1966080
  98.9 131.6 %all-gather.9.cloned.1.call-start = ((), (), s32[]{:S(2)}) async-start(), calls=%async_computation.8 | async-start | bytes 7864320 | tf_op jit(solution)/shard_map/all_gather | solution.py:43
  113.0 156.0 %all-gather.5.cloned.1.call-start = ((), (), s32[]{:S(2)}) async-start(), calls=%async_computation.6 | async-start | bytes 1966080 | tf_op jit(solution)/shard_map/all_gather | solution.py:66
  238.2 63.3 %all-gather.7.cloned.1.call-start = ((), (), s32[]{:S(2)}) async-start(), calls=%async_computation.7 | async-start | bytes 1966080 | tf_op jit(solution)/shard_map/all_gather | solution.py:67
  253.8 64.4 %all-to-all-start.1 = ((bf16[8,64,1024]{2,0,1:T(8,128)(2,1)}), bf16[8,64,1024]{2,0,1:T(8,128)(2,1)}, u32[]{:S(2)}, u32[]{:S(2)}) async-start(bf16[8,64,1024]{2,0,1:T(8,128)(2,1)} %copy.51), calls=%async_computation.1 | async-start | bytes 2097152 | tf_op jit(solution)/shard_map/all_to_all | solution.py:74
  318.2 31.3 %all-to-all-start.3 = ((bf16[8,64,1024]{2,0,1:T(8,128)(2,1)}), bf16[8,64,1024]{2,0,1:T(8,128)(2,1)}, u32[]{:S(2)}, u32[]{:S(2)}) async-start(bf16[8,64,1024]{2,0,1:T(8,128)(2,1)} %copy.55), calls=%async_computation.3 | async-start | bytes 2097152 | tf_op jit(solution)/shard_map/all_to_all | solution.py:75
  336.6 15.6 %copy-start.1 = (bf16[32,1024]{1,0:T(8,128)(2,1)S(1)}, bf16[32,1024]{1,0:T(8,128)(2,1)}, u32[]{:S(2)}) copy-start(bf16[32,1024]{1,0:T(8,128)(2,1)} %param.7) | copy-start | bytes 196612
Sparse Core Ops, SparseCore 0:
  62.3 62.0 all-reduce.1
  127.4 31.1 reduce-scatter.3
  160.4 70.0 all-gather.8
  238.3 30.6 all-gather.4
  270.7 30.6 all-gather.6
